TPU v7x, 128 devices: a whole 4x4x4 slice. The times are simulated.
128 devices in a mesh: users: 16 (over x, y), items: 8 (over z, core).
Axes of the slice: x: 4, y: 4, z: 4, core: 2. Of those that a mesh axis runs over, the one named last changes fastest.
Arguments:
- tiles: float32 [16, 8, 4, 32, 128, 128], P('users', 'items'), may hold values from -6 to 6
- user_blocks: int32 [16, 8, 4], P('users', 'items'), may hold values from 0 to 15, as said below
- item_blocks: int32 [16, 8, 4], P('users', 'items'), may hold values from 0 to 127, as said below
- counts: int32 [16, 8], P('users', 'items'), may hold values from 1 to 4, as said below
- user_factor: float32 [64, 32768], P(None, ('users', 'items')), may hold values from -0.5 to 0.5
- item_factor: float32 [64, 131072], P(None, ('items', 'users')), may hold values from -0.5 to 0.5
- week_factor: float32 [32, 64], replicated, may hold values from -1 to 1
Outputs:
- m_users: float32 [64, 32768], P(None, ('users', 'items'))
- m_items: float32 [64, 131072], P(None, ('items', 'users'))
Inputs may be any that keep to these rules, and one draw needn't show every extreme that they name: `user_blocks`: within one device the first 4 slots name distinct (user block, item block) pairs of its grid row and grid column. `item_blocks`: paired with user_blocks slot by slot. `counts`: some device holds 4 tiles in every draw.
All inputs are finite; a program needn't handle non-finite values.
Results may differ from a plain program's by a relative error of at most 0.0001.
Values sent between devices are 32-bit elements; how exact they have to be, the bound alone decides.
A program may use at most 128 MiB of HBM per device.

v0:
```python
import jax
import jax.numpy as jnp
import numpy as np
from jax import lax
from jax.sharding import Mesh
from jax.sharding import PartitionSpec as P

HIGHEST = lax.Precision.HIGHEST


def on_device(tiles, user_blocks, item_blocks, counts, user_factor, item_factor, week_factor):
    x_size = lax.axis_size("ux")
    slot_total = tiles.shape[2]
    user_width = tiles.shape[4]
    item_width = tiles.shape[5]
    rank_size = week_factor.shape[1]
    me_x = lax.axis_index("ux")
    user_ids = user_blocks[0, 0]
    item_ids = item_blocks[0, 0]
    live = (jnp.arange(slot_total, dtype=jnp.int32) < counts[0, 0]).astype(jnp.float32)
    user_rows = lax.all_gather(user_factor, ("iz", "ic"), axis=1, tiled=True)
    user_block_total = user_rows.shape[1] // user_width
    user_rows = user_rows.reshape(rank_size, user_block_total, user_width)
    user_hot = (user_ids[:, None] == jnp.arange(user_block_total, dtype=jnp.int32)[None, :]).astype(
        jnp.float32
    )
    user_sel = jnp.einsum("sn,rna->sra", user_hot, user_rows, precision=HIGHEST)
    group_rows = lax.all_gather(item_factor, "uy", axis=1, tiled=True)
    group_blocks = group_rows.shape[1] // item_width
    group_rows = group_rows.reshape(rank_size, group_blocks, item_width)
    wanted = lax.all_gather(item_ids, "ux", axis=0, tiled=False)
    owner_group = wanted // group_blocks
    local_block = wanted % group_blocks
    send_hot = jnp.where(
        (owner_group == me_x)[:, :, None],
        (
            local_block[:, :, None] == jnp.arange(group_blocks, dtype=jnp.int32)[None, None, :]
        ).astype(jnp.float32),
        0.0,
    )
    send = jnp.einsum("xsl,rlb->xsrb", send_hot, group_rows, precision=HIGHEST)
    item_sel = lax.psum_scatter(send, "ux", scatter_dimension=0, tiled=True)[0]
    data = tiles[0, 0]
    by_items = jnp.einsum("skab,srb->srka", data, item_sel, precision=HIGHEST)
    user_terms = (
        jnp.einsum("srka,kr->sra", by_items, week_factor, precision=HIGHEST) * live[:, None, None]
    )
    by_users = jnp.einsum("skab,sra->srkb", data, user_sel, precision=HIGHEST)
    item_terms = (
        jnp.einsum("srkb,kr->srb", by_users, week_factor, precision=HIGHEST) * live[:, None, None]
    )
    part_users = jnp.einsum("sn,sra->rna", user_hot, user_terms, precision=HIGHEST).reshape(
        rank_size, user_block_total * user_width
    )
    m_users = lax.psum_scatter(part_users, ("iz", "ic"), scatter_dimension=1, tiled=True)
    all_terms = lax.all_gather(item_terms, "ux", axis=0, tiled=False)
    take_hot = jnp.where(
        (owner_group == me_x)[:, :, None],
        (
            local_block[:, :, None] == jnp.arange(group_blocks, dtype=jnp.int32)[None, None, :]
        ).astype(jnp.float32),
        0.0,
    )
    part_items = jnp.einsum("xsl,xsrb->rlb", take_hot, all_terms, precision=HIGHEST).reshape(
        rank_size, group_blocks * item_width
    )
    m_items = lax.psum_scatter(part_items, "uy", scatter_dimension=1, tiled=True)
    del x_size
    return (m_users, m_items)


def solution(mesh):
    users, items = (mesh.shape["users"], mesh.shape["items"])
    devices = np.asarray(mesh.devices).reshape(users // 4, 4, items // 2, 2)
    fine = Mesh(devices, ("ux", "uy", "iz", "ic"))
    rows = ("ux", "uy")
    cols = ("iz", "ic")
    return jax.shard_map(
        on_device,
        mesh=fine,
        in_specs=(
            P(rows, cols, None, None, None, None),
            P(rows, cols, None),
            P(rows, cols, None),
            P(rows, cols),
            P(None, rows + cols),
            P(None, cols + rows),
            P(),
        ),
        out_specs=(P(None, rows + cols), P(None, cols + rows)),
        check_vma=False,
    )
```

profile of v0, /device:TPU:0, one launch (start us, length us, event | category | flops | bytes accessed | tf_op | source)
XLA Modules:
  0.0 142.8 jit_solution(14950030643989074315)
XLA Ops:
  7.2 0.7 all-gather.4.cloned.1.call-update
  8.0 9.9 %all-gather = s32[4,1,4]{2,1,0:T(1,128)S(1)} all-gather(s32[1,1,4]{2,1,0:T(1,128)} %param.9), channel_id=2, replica_groups=mesh['ux'=4,'uy'=4,'iz'=4,'ic'=2] {'ux'}, dimensions={0}, use_global_device_ids=true | all-gather | bytes 80 | tf_op jit(solution)/shard_map/all_gather | solution.py:31
  17.9 0.1 copy.18
  18.0 0.1 copy.17
  18.8 14.5 %all_gather.17 = f32[64,2048]{1,0:T(8,128)S(1)} all-gather(f32[64,256]{1,0:T(8,128)} %param.11), channel_id=1, replica_groups=mesh['ux'=4,'uy'=4,'iz'=4,'ic'=2] {'iz','ic'}, dimensions={1}, use_global_device_ids=true | all-gather | bytes 589824 | tf_op jit(solution)/shard_map/all_gather | solution.py:21
  33.3 2.9 %all-gather.4.cloned.1.call-done = f32[64,4096]{1,0:T(8,128)} async-done(((f32[64,1024]{1,0:T(8,128)}), f32[64,4096]{1,0:T(8,128)}) %all-gather.4.cloned.1.call-update) | async-done | bytes 1048592 | tf_op jit(solution)/shard_map/all_gather | solution.py:28
  36.2 1.4 copy.39
  37.6 0.8 fusion.16
  38.4 0.8 copy.20
  39.4 0.1 copy.41
  39.5 0.3 convolution_bitcast_fusion
  39.9 6.8 %fusion = f32[4,64,32,128]{3,1,2,0:T(8,128)S(1)} fusion(f32[1,1,4,32,128,128]{5,4,3,2,1,0:T(8,128)} %param.7, f32[4,64,128,1]{2,0,1,3:T(4,128)S(1)} %convolution_bitcast_fusion), kind=kOutput, calls=%fused_computation | convolution fusion | flops 1610612736 | bytes 12713984 | tf_op jit(solution)/shard_map/skab,sra->srkb/dot_general | solution.py:48
  46.7 5.7 %fusion.4 = f32[64,1,4,128]{3,1,2,0:T(1,128)S(1)} fusion(f32[32,64,1,1]{0,2,3,1:T(1,128)S(1)} %copy.28, f32[4,64,32,128]{3,1,2,0:T(8,128)S(1)} %fusion), kind=kOutput, calls=%fused_computation.4 | convolution fusion | flops 12582912 | bytes 4333568 | tf_op jit(solution)/shard_map/srkb,kr->srb/dot_general | solution.py:50
  52.3 8.8 %reduce-scatter.4.cloned.1.call-done = f32[1,4,64,128]{3,2,1,0:T(8,128)} async-done(((f32[4,4,64,128]{3,2,1,0:T(8,128)}), f32[1,4,64,128]{3,2,1,0:T(8,128)}) %reduce-scatter.4.cloned.1.call-update) | async-done | bytes 131088 | tf_op jit(solution)/shard_map/reduce_scatter | solution.py:42
  61.1 11.7 %fusion.2 = f32[4,64,32,128]{3,1,2,0:T(8,128)S(1)} fusion(f32[1,1,4,32,128,128]{5,4,3,2,1,0:T(8,128)} %param.7, f32[1,4,64,128]{3,2,1,0:T(8,128)} %reduce-scatter.4.cloned.1.call-done), kind=kOutput, calls=%fused_computation.2 | convolution fusion | flops 1610612736 | bytes 12713984 | tf_op jit(solution)/shard_map/skab,srb->srka/dot_general | solution.py:44
  72.7 5.7 %fusion.6 = f32[64,1,4,128]{3,1,2,0:T(1,128)S(1)} fusion(f32[32,64,1,1]{0,2,3,1:T(1,128)S(1)} %copy.28, f32[4,64,32,128]{3,1,2,0:T(8,128)S(1)} %fusion.2), kind=kOutput, calls=%fused_computation.6 | convolution fusion | flops 12582912 | bytes 4333568 | tf_op jit(solution)/shard_map/srka,kr->sra/dot_general | solution.py:46
  78.4 0.1 fusion.11
  78.5 0.5 fusion.14
  79.0 1.0 copy.58
  80.0 12.8 %all-gather.1 = f32[16,64,128]{2,1,0:T(8,128)S(1)} all-gather(f32[4,64,128]{2,1,0:T(8,128)S(1)} %get-tuple-element.2), channel_id=3, replica_groups=mesh['ux'=4,'uy'=4,'iz'=4,'ic'=2] {'ux'}, dimensions={0}, use_global_device_ids=true | all-gather | bytes 655360 | tf_op jit(solution)/shard_map/all_gather | solution.py:56
  92.8 1.4 fusion.8
  94.2 1.6 %copy.57 = f32[8,8,32,128]{3,1,2,0:T(8,128)} copy(f32[8,8,32,128]{3,2,1,0:T(8,128)S(1)} %bitcast.67) | data formatting | bytes 2097152
  95.8 15.2 %reduce-scatter.6.cloned.1.call-done = f32[64,256]{1,0:T(8,128)} async-done(((f32[64,2048]{1,0:T(8,128)}), f32[64,256]{1,0:T(8,128)}) %reduce-scatter.6.cloned.1.call-update) | async-done | bytes 65552 | tf_op jit(solution)/shard_map/reduce_scatter | solution.py:55
  111.1 25.2 %reduce-scatter.8.cloned.1.call-done = f32[64,1024]{1,0:T(8,128)} async-done(((f32[64,4096]{1,0:T(8,128)}), f32[64,1024]{1,0:T(8,128)}) %reduce-scatter.8.cloned.1.call-update) | async-done | bytes 262160 | tf_op jit(solution)/shard_map/reduce_scatter | solution.py:67
  (15 shorter events, 0.3 us)
Async XLA Ops:
  7.2 32.2 %copy-start = (f32[32,64]{1,0:T(8,128)S(1)}, f32[32,64]{1,0:T(8,128)}, u32[]{:S(2)}) copy-start(f32[32,64]{1,0:T(8,128)} %param.13) | copy-start | bytes 24580
  7.2 32.4 %copy-start.1 = (s32[1,1,4]{2,1,0:T(1,128)S(1)}, s32[1,1,4]{2,1,0:T(1,128)}, u32[]{:S(2)}) copy-start(s32[1,1,4]{2,1,0:T(1,128)} %param.8) | copy-start | bytes 52
  7.2 29.0 %all-gather.4.cloned.1.call-start = ((), (), s32[]{:S(2)}) async-start(), calls=%async_computation.3 | async-start | bytes 1310720 | tf_op jit(solution)/shard_map/all_gather | solution.py:28
  7.9 53.2 %reduce-scatter.4.cloned.1.call-start = ((), (), s32[]{:S(2)}) async-start(), calls=%async_computation.4 | async-start | bytes 655360 | tf_op jit(solution)/shard_map/reduce_scatter | solution.py:42
  39.3 71.8 %reduce-scatter.6.cloned.1.call-start = ((), (), s32[]{:S(2)}) async-start(), calls=%async_computation.5 | async-start | bytes 589824 | tf_op jit(solution)/shard_map/reduce_scatter | solution.py:55
  80.0 56.3 %reduce-scatter.8.cloned.1.call-start = ((), (), s32[]{:S(2)}) async-start(), calls=%async_computation.6 | async-start | bytes 1310720 | tf_op jit(solution)/shard_map/reduce_scatter | solution.py:67
Sparse Core Ops, SparseCore 0:
  9.7 26.4 all-gather.3
  39.4 21.6 reduce-scatter.3
  80.1 30.9 reduce-scatter.5
  114.0 22.1 reduce-scatter.7
where the time goes:
time: 143 us
  waiting for transfers between devices  52.8 us (37%)
  blocking collectives  37.2 us (26%)
  matrix products  32.8 us (23%)
  between operations  14.5 us (10%)
  local copies, waits for them, and re-layouts  5.19 us (4%)
    reduce_scatter x1, waiting for transfers between devices, on_device(): lax.psum_scatter(part_items, 'uy', scatter_dimension=1, tiled=True)  25.2 us
    reduce_scatter x1, waiting for transfers between devices, on_device(): lax.psum_scatter(part_users, ('iz', 'ic'), scatter_dimension=1, tiled=True)  15.2 us
    all_gather x1, blocking collectives, on_device(): user_rows = lax.all_gather(user_factor, ('iz', 'ic'), axis=1, tiled=True)  14.5 us
    all_gather x1, blocking collectives, on_device(): all_terms = lax.all_gather(item_terms, 'ux', axis=0, tiled=False)  12.8 us
    dot_general x1, matrix products, on_device(): by_items = jnp.einsum('skab,srb->srka', data, item_sel, precision=HIGHEST)  11.7 us
    all_gather x1, blocking collectives, on_device(): wanted = lax.all_gather(item_ids, 'ux', axis=0, tiled=False)  9.92 us
    reduce_scatter x1, waiting for transfers between devices, on_device(): item_sel = lax.psum_scatter(send, 'ux', scatter_dimension=0, tiled=True)[0]  8.75 us
    dot_general x1, matrix products, on_device(): by_users = jnp.einsum('skab,sra->srkb', data, user_sel, precision=HIGHEST)  6.8 us
  transfers between devices with their start and end apart: 4, of which 4 were waited for; matrix products, arithmetic and copies ran while one was open for 11% of the time, Pallas kernels for 0%

commit v1 on v0

--- a/solution.py
+++ b/solution.py
@@ -25,7 +25,9 @@
         jnp.float32
     )
     user_sel = jnp.einsum("sn,rna->sra", user_hot, user_rows, precision=HIGHEST)
-    group_rows = lax.all_gather(item_factor, "uy", axis=1, tiled=True)
+    group_rows = jnp.concatenate(
+        lax.all_to_all(jnp.stack([item_factor] * lax.axis_size("uy")), "uy", 0, 0), axis=1
+    )
     group_blocks = group_rows.shape[1] // item_width
     group_rows = group_rows.reshape(rank_size, group_blocks, item_width)
     wanted = lax.all_gather(item_ids, "ux", axis=0, tiled=False)

time: 143 us -> 145 us (1.014)
  starting transfers between devices: 0.16 us -> 4.81 us
  waiting for transfers between devices: 52.8 us -> 48.3 us
  local copies, waits for them, and re-layouts: 5.19 us -> 6.92 us
    all_to_all x0 -> x1, starting transfers between devices: none -> 4.55 us  [on_device(): lax.all_to_all(jnp.stack([item_factor] * lax.axis_size('uy')), 'uy', 0, 0)]
    all_gather x1 -> x0, waiting for transfers between devices: 2.87 us -> none  [on_device(): group_rows = lax.all_gather(item_factor, 'uy', axis=1, tiled=True)]
    another operation x0 -> x2, local copies, waits for them, and re-layouts: none -> 2.46 us  [the longest x1 2.04 us: on_device(): jnp.stack([item_factor] * lax.axis_size('uy'))]
    unnamed x9 -> x8, local copies, waits for them, and re-layouts: 4.14 us -> 2.73 us
  transfers between devices with their start and end apart: 4 -> 4, of which waited for: 4 -> 3; matrix products, arithmetic and copies ran while one was open for 11% -> 11% of each run, Pallas kernels for 0% -> 0%
where the time goes in v1:
time: 145 us
  waiting for transfers between devices  48.3 us (33%)
  blocking collectives  37.3 us (26%)
  matrix products  32.8 us (23%)
  between operations  14.5 us (10%)
  local copies, waits for them, and re-layouts  6.92 us (5%)
  starting transfers between devices  4.81 us (3%)
    reduce_scatter x1, waiting for transfers between devices, on_device(): lax.psum_scatter(part_items, 'uy', scatter_dimension=1, tiled=True)  25.4 us
    reduce_scatter x1, waiting for transfers between devices, on_device(): lax.psum_scatter(part_users, ('iz', 'ic'), scatter_dimension=1, tiled=True)  15.2 us
    all_gather x1, blocking collectives, on_device(): user_rows = lax.all_gather(user_factor, ('iz', 'ic'), axis=1, tiled=True)  14.5 us
    all_gather x1, blocking collectives, on_device(): all_terms = lax.all_gather(item_terms, 'ux', axis=0, tiled=False)  12.8 us
    dot_general x1, matrix products, on_device(): by_items = jnp.einsum('skab,srb->srka', data, item_sel, precision=HIGHEST)  11.7 us
    all_gather x1, blocking collectives, on_device(): wanted = lax.all_gather(item_ids, 'ux', axis=0, tiled=False)  9.96 us
    reduce_scatter x1, waiting for transfers between devices, on_device(): item_sel = lax.psum_scatter(send, 'ux', scatter_dimension=0, tiled=True)[0]  7.62 us
    dot_general x1, matrix products, on_device(): by_users = jnp.einsum('skab,sra->srkb', data, user_sel, precision=HIGHEST)  6.8 us
  transfers between devices with their start and end apart: 4, of which 3 were waited for; matrix products, arithmetic and copies ran while one was open for 11% of the time, Pallas kernels for 0%

profile of v1, /device:TPU:0, one launch (start us, length us, event | category | flops | bytes accessed | tf_op | source)
XLA Modules:
  0.0 144.7 jit_solution(18037326689378226074)
XLA Ops:
  7.2 2.0 %stack.2 = f32[4,64,1024]{2,1,0:T(8,128)} broadcast(f32[64,1024]{1,0:T(8,128)} %param.12), dimensions={1,2} | broadcast | bytes 1310720 | tf_op jit(solution)/shard_map/stack | solution.py:29
  9.2 4.5 %all-to-all-start = ((f32[4,64,1024]{2,1,0:T(8,128)}), f32[4,64,1024]{2,1,0:T(8,128)S(1)}, u32[]{:S(2)}, u32[]{:S(2)}) async-start(f32[4,64,1024]{2,1,0:T(8,128)} %stack.2), calls=%async_computation | async-start | bytes 2097152 | tf_op jit(solution)/shard_map/all_to_all | solution.py:29
  13.8 10.0 %all-gather = s32[4,1,4]{2,1,0:T(1,128)S(1)} all-gather(s32[1,1,4]{2,1,0:T(1,128)} %param.9), channel_id=2, replica_groups=mesh['ux'=4,'uy'=4,'iz'=4,'ic'=2] {'ux'}, dimensions={0}, use_global_device_ids=true | all-gather | bytes 80 | tf_op jit(solution)/shard_map/all_gather | solution.py:33
  23.7 0.1 copy.18
  23.8 0.1 copy.17
  24.6 14.5 %all_gather.13 = f32[64,2048]{1,0:T(8,128)S(1)} all-gather(f32[64,256]{1,0:T(8,128)} %param.11), channel_id=1, replica_groups=mesh['ux'=4,'uy'=4,'iz'=4,'ic'=2] {'iz','ic'}, dimensions={1}, use_global_device_ids=true | all-gather | bytes 589824 | tf_op jit(solution)/shard_map/all_gather | solution.py:21
  39.1 0.7 copy.19
  39.8 0.4 reshape.33
  40.2 0.8 fusion.16
  41.1 0.8 copy.21
  41.9 0.2 reduce-scatter.6.cloned.1.call-start
  42.4 0.3 convolution_bitcast_fusion
  42.7 6.8 %fusion = f32[4,64,32,128]{3,1,2,0:T(8,128)S(1)} fusion(f32[1,1,4,32,128,128]{5,4,3,2,1,0:T(8,128)} %param.7, f32[4,64,128,1]{2,0,1,3:T(4,128)S(1)} %convolution_bitcast_fusion), kind=kOutput, calls=%fused_computation | convolution fusion | flops 1610612736 | bytes 12713984 | tf_op jit(solution)/shard_map/skab,sra->srkb/dot_general | solution.py:50
  49.5 5.7 %fusion.4 = f32[64,1,4,128]{3,1,2,0:T(1,128)S(1)} fusion(f32[32,64,1,1]{0,2,3,1:T(1,128)S(1)} %copy.29, f32[4,64,32,128]{3,1,2,0:T(8,128)S(1)} %fusion), kind=kOutput, calls=%fused_computation.4 | convolution fusion | flops 12582912 | bytes 4333568 | tf_op jit(solution)/shard_map/srkb,kr->srb/dot_general | solution.py:52
  55.2 7.6 %reduce-scatter.4.cloned.1.call-done = f32[1,4,64,128]{3,2,1,0:T(8,128)} async-done(((f32[4,4,64,128]{3,2,1,0:T(8,128)}), f32[1,4,64,128]{3,2,1,0:T(8,128)}) %reduce-scatter.4.cloned.1.call-update) | async-done | bytes 131088 | tf_op jit(solution)/shard_map/reduce_scatter | solution.py:44
  62.8 11.7 %fusion.2 = f32[4,64,32,128]{3,1,2,0:T(8,128)S(1)} fusion(f32[1,1,4,32,128,128]{5,4,3,2,1,0:T(8,128)} %param.7, f32[1,4,64,128]{3,2,1,0:T(8,128)} %reduce-scatter.4.cloned.1.call-done), kind=kOutput, calls=%fused_computation.2 | convolution fusion | flops 1610612736 | bytes 12713984 | tf_op jit(solution)/shard_map/skab,srb->srka/dot_general | solution.py:46
  74.5 5.7 %fusion.6 = f32[64,1,4,128]{3,1,2,0:T(1,128)S(1)} fusion(f32[32,64,1,1]{0,2,3,1:T(1,128)S(1)} %copy.29, f32[4,64,32,128]{3,1,2,0:T(8,128)S(1)} %fusion.2), kind=kOutput, calls=%fused_computation.6 | convolution fusion | flops 12582912 | bytes 4333568 | tf_op jit(solution)/shard_map/srka,kr->sra/dot_general | solution.py:48
  80.2 0.5 fusion.14
  80.7 1.0 copy.58
  81.8 12.8 %all-gather.1 = f32[16,64,128]{2,1,0:T(8,128)S(1)} all-gather(f32[4,64,128]{2,1,0:T(8,128)S(1)} %get-tuple-element.2), channel_id=3, replica_groups=mesh['ux'=4,'uy'=4,'iz'=4,'ic'=2] {'ux'}, dimensions={0}, use_global_device_ids=true | all-gather | bytes 655360 | tf_op jit(solution)/shard_map/all_gather | solution.py:58
  94.5 1.4 fusion.8
  95.9 1.6 %copy.57 = f32[8,8,32,128]{3,1,2,0:T(8,128)} copy(f32[8,8,32,128]{3,2,1,0:T(8,128)S(1)} %bitcast.65) | data formatting | bytes 2097152
  97.5 15.2 %reduce-scatter.6.cloned.1.call-done = f32[64,256]{1,0:T(8,128)} async-done(((f32[64,2048]{1,0:T(8,128)}), f32[64,256]{1,0:T(8,128)}) %reduce-scatter.6.cloned.1.call-update) | async-done | bytes 65552 | tf_op jit(solution)/shard_map/reduce_scatter | solution.py:57
  112.7 25.4 %reduce-scatter.8.cloned.1.call-done = f32[64,1024]{1,0:T(8,128)} async-done(((f32[64,4096]{1,0:T(8,128)}), f32[64,1024]{1,0:T(8,128)}) %reduce-scatter.8.cloned.1.call-update) | async-done | bytes 262160 | tf_op jit(solution)/shard_map/reduce_scatter | solution.py:69
  (16 shorter events, 0.4 us)
Async XLA Ops:
  9.2 29.9 %all-to-all-start = ((f32[4,64,1024]{2,1,0:T(8,128)}), f32[4,64,1024]{2,1,0:T(8,128)S(1)}, u32[]{:S(2)}, u32[]{:S(2)}) async-start(f32[4,64,1024]{2,1,0:T(8,128)} %stack.2), calls=%async_computation | async-start | bytes 2097152 | tf_op jit(solution)/shard_map/all_to_all | solution.py:29
  13.8 28.4 %copy-start = (f32[32,64]{1,0:T(8,128)S(1)}, f32[32,64]{1,0:T(8,128)}, u32[]{:S(2)}) copy-start(f32[32,64]{1,0:T(8,128)} %param.13) | copy-start | bytes 24580
  13.8 49.0 %reduce-scatter.4.cloned.1.call-start = ((), (), s32[]{:S(2)}) async-start(), calls=%async_computation.4 | async-start | bytes 655360 | tf_op jit(solution)/shard_map/reduce_scatter | solution.py:44
  39.1 3.2 %copy-start.1 = (s32[1,1,4]{2,1,0:T(1,128)S(1)}, s32[1,1,4]{2,1,0:T(1,128)}, u32[]{:S(2)}) copy-start(s32[1,1,4]{2,1,0:T(1,128)} %param.8) | copy-start | bytes 52
  41.9 70.8 %reduce-scatter.6.cloned.1.call-start = ((), (), s32[]{:S(2)}) async-start(), calls=%async_computation.5 | async-start | bytes 589824 | tf_op jit(solution)/shard_map/reduce_scatter | solution.py:57
  81.7 56.5 %reduce-scatter.8.cloned.1.call-start = ((), (), s32[]{:S(2)}) async-start(), calls=%async_computation.6 | async-start | bytes 1310720 | tf_op jit(solution)/shard_map/reduce_scatter | solution.py:69
Sparse Core Ops, SparseCore 0:
  42.0 20.6 reduce-scatter.3
  81.8 30.8 reduce-scatter.5
  115.9 22.2 reduce-scatter.7
